TPU v7x, 32 devices: a whole 2x2x4 slice. The times are simulated.
32 devices in a mesh: pitch: 2 (over core), axial: 4 (over y, x), span: 4 (over z).
Axes of the slice: x: 2, y: 2, z: 4, core: 2. Of those that a mesh axis runs over, the one named last changes fastest.
Arguments:
- state: float32 [5, 16, 128, 512], P(None, 'pitch', 'axial', 'span'), as said below
- coeffs: float32 [2, 4, 5, 128, 512], P(None, None, None, 'axial', 'span'), may hold values from -3 to 3
- lag_shift: int32 [1], replicated, may hold values from 0 to 63
- harmonics: int32 [512], P('span'), may hold values from 1 to 4
Outputs:
- new_state: float32 [5, 16, 128, 512], P(None, 'pitch', 'axial', 'span')
Inputs may be any that keep to these rules, and one draw needn't show every extreme that they name: `state`: density lies in 0.8 to 1.25, momenta within -1.5 to 1.5, total energy within 1.6 to 3.4.
All inputs are finite; a program needn't handle non-finite values.
Results may differ from a plain program's by a relative error of at most 0.0001.
Values sent between devices are 32-bit elements; how exact they have to be, the bound alone decides.
A program may use at most 64 MiB of HBM per device.

v0:
```python
import math
import jax
import jax.numpy as jnp
from jax import lax
from jax.sharding import PartitionSpec as P

HARM_MAX = 4
PERIOD_SAMPLES = 64
HEAT_RATIO_GAS = 1.4
STEP_RATE = 0.25
DAMPING = 0.5
STENCIL = (1.0, -8.0, 28.0, -56.0, 70.0, -56.0, 28.0, -8.0, 1.0)


def padded(cells, sides, width, closed):
    for axis, dim in sides:
        count = lax.axis_size(axis)
        ends = count if closed else count - 1
        head = lax.slice_in_dim(cells, 0, width, axis=dim)
        tail = lax.slice_in_dim(cells, cells.shape[dim] - width, cells.shape[dim], axis=dim)
        cells = jnp.concatenate(
            [
                lax.ppermute(tail, axis, [(i, (i + 1) % count) for i in range(ends)]),
                cells,
                lax.ppermute(head, axis, [((i + 1) % count, i) for i in range(ends)]),
            ],
            axis=dim,
        )
    return cells


def pitch_flux(state):
    density = state[0]
    speed = state[2] / density
    kinetic = 0.5 * (state[1] * state[1] + state[2] * state[2] + state[3] * state[3]) / density
    pressure = (HEAT_RATIO_GAS - 1.0) * (state[4] - kinetic)
    return jnp.stack(
        [
            state[2],
            state[1] * speed,
            state[2] * speed + pressure,
            state[3] * speed,
            (state[4] + pressure) * speed,
        ]
    )


def seam_jump(coeffs, lag_shift, harmonics):
    order = jnp.arange(HARM_MAX)
    phase = (
        2.0
        * math.pi
        / PERIOD_SAMPLES
        * (order + 1).astype(jnp.float32)
        * lag_shift[0].astype(jnp.float32)
    )
    active = (order[:, None] < harmonics[None, :]).astype(jnp.float32)
    cosine = active * jnp.cos(phase)[:, None]
    sine = active * jnp.sin(phase)[:, None]
    first = jnp.sum(cosine[:, None, None, :] * coeffs[0], axis=0)
    second = jnp.sum(sine[:, None, None, :] * coeffs[1], axis=0)
    return first + second


def damping_from(extended, naxial, nspan):
    along = jnp.zeros_like(extended[:, :, 4 : 4 + naxial, 4 : 4 + nspan])
    across = jnp.zeros_like(along)
    for displacement in range(9):
        along = (
            along
            + STENCIL[displacement]
            * extended[:, :, displacement : displacement + naxial, 4 : 4 + nspan]
        )
        across = (
            across
            + STENCIL[displacement]
            * extended[:, :, 4 : 4 + naxial, displacement : displacement + nspan]
        )
    return (along + across) / 256.0


def signed_power(base, count):
    magnitude = jnp.power(jnp.float32(abs(base)), jnp.asarray(count).astype(jnp.float32))
    if base < 0.0:
        magnitude = magnitude * (1 - 2 * (jnp.asarray(count) % 2)).astype(jnp.float32)
    return magnitude


def line_root(main_band_coefficient, neighbour_band_coefficient):
    characteristic_polynomial_radicand = math.sqrt(
        main_band_coefficient * main_band_coefficient
        - 4.0 * neighbour_band_coefficient * neighbour_band_coefficient
    )
    recurrence_decay_number = (-main_band_coefficient + characteristic_polynomial_radicand) / (
        2.0 * neighbour_band_coefficient
    )
    return (
        recurrence_decay_number,
        1.0 / (main_band_coefficient + 2.0 * neighbour_band_coefficient * recurrence_decay_number),
    )


def edge_sums(values, recurrence_decay_number):
    pitch_cells = values.shape[1]
    cell_pos = jnp.arange(pitch_cells)
    tail_part = jnp.einsum(
        "j,fjas->fas",
        signed_power(recurrence_decay_number, pitch_cells - 1 - cell_pos),
        values,
        precision=lax.Precision.HIGHEST,
    )
    head_part = jnp.einsum(
        "j,fjas->fas",
        signed_power(recurrence_decay_number, cell_pos),
        values,
        precision=lax.Precision.HIGHEST,
    )
    return (tail_part, head_part)


def factor_root_weights(step_decays, count):
    return jnp.stack(
        [signed_power(step_decays[0], count), signed_power(step_decays[1], count)], axis=-1
    )


def finish(values, recurrence_decay_number, scale_value, carry_up, carry_down):
    pitch_cells = values.shape[1]
    cell_pos = jnp.arange(pitch_cells)
    kernel = signed_power(recurrence_decay_number, jnp.abs(cell_pos[:, None] - cell_pos[None, :]))
    solved = jnp.einsum("ij,fjas->fias", kernel, values, precision=lax.Precision.HIGHEST)
    enter_weights = signed_power(recurrence_decay_number, cell_pos + 1)
    leave_weights = signed_power(recurrence_decay_number, pitch_cells - cell_pos)
    solved = (
        solved
        + enter_weights[None, :, None, None] * carry_up[:, None]
        + leave_weights[None, :, None, None] * carry_down[:, None]
    )
    return scale_value * solved


def shards(state, coeffs, lag_shift, harmonics):
    flux = pitch_flux(state)
    jump = seam_jump(coeffs, lag_shift, harmonics)
    npitch = lax.axis_size("pitch")
    position = lax.axis_index("pitch")
    at_first = jnp.where(position == 0, 1.0, 0.0).astype(jnp.float32)
    at_last = jnp.where(position == npitch - 1, 1.0, 0.0).astype(jnp.float32)
    widened = padded(flux, (("pitch", 1),), 1, True)
    rhs = 0.75 * (widened[:, 2:] - widened[:, :-2])
    rhs = rhs.at[:, 0].add(0.75 * (at_first * jump))
    rhs = rhs.at[:, -1].add(0.75 * (at_last * jump))
    pitch_cells = rhs.shape[1]
    pitch_total = pitch_cells * npitch
    diffusion = float(pitch_total * pitch_total // 64)
    compact_root, compact_scale = line_root(1.0, 0.25)
    relax_root, relax_scale = line_root(1.0 + 2.0 * diffusion, -diffusion)
    tail_compact, head_compact = edge_sums(rhs, compact_root)
    tail_relax, head_relax = edge_sums(state, relax_root)
    tail_sums = jnp.stack([tail_compact, tail_relax])
    leading_partial_totals = jnp.stack([head_compact, head_relax])
    step_decays = (compact_root**pitch_cells, relax_root**pitch_cells)
    wrap_factors = jnp.array(
        [1.0 / (1.0 - step_decays[0] ** npitch), 1.0 / (1.0 - step_decays[1] ** npitch)],
        jnp.float32,
    )
    collected = (
        lax.all_gather(tail_sums[None], "pitch", axis=0, tiled=True),
        lax.all_gather(leading_partial_totals[None], "pitch", axis=0, tiled=True),
    )
    others = jnp.arange(npitch)
    up_weights = (
        factor_root_weights(step_decays, (position - 1 - others) % npitch) * wrap_factors[None, :]
    )
    descending_sweep_multipliers = (
        factor_root_weights(step_decays, (others - position - 1) % npitch) * wrap_factors[None, :]
    )
    carry_up = jnp.einsum(
        "er,erfas->rfas", up_weights, collected[0], precision=lax.Precision.HIGHEST
    )
    carry_down = jnp.einsum(
        "er,erfas->rfas",
        descending_sweep_multipliers,
        collected[1],
        precision=lax.Precision.HIGHEST,
    )
    deriv = finish(rhs, compact_root, compact_scale, carry_up[0], carry_down[0])
    smoothed_increment = finish(state, relax_root, relax_scale, carry_up[1], carry_down[1])
    extended = padded(state, (("axial", 2), ("span", 3)), 4, False)
    damp = damping_from(extended, state.shape[2], state.shape[3])
    return smoothed_increment - STEP_RATE * deriv - DAMPING * damp


def solution(mesh):
    placed = (
        P(None, "pitch", "axial", "span"),
        P(None, None, None, "axial", "span"),
        P(),
        P("span"),
    )
    return jax.shard_map(
        shards,
        mesh=mesh,
        in_specs=placed,
        out_specs=P(None, "pitch", "axial", "span"),
        check_vma=False,
    )
```

profile of v0, /device:TPU:12, one launch (start us, length us, event | category | flops | bytes accessed | tf_op | source)
XLA Modules:
  0.0 47.0 jit_solution(12623928123771898618)
XLA Ops:
  0.0 1.0 %slice_dynamic-update-slice_fusion = f32[5,8,32,128]{3,2,1,0:T(8,128)S(1)} fusion(f32[5,8,32,128]{3,2,1,0:T(8,128)} %param.9), kind=kLoop, calls=%fused_computation.85 | loop fusion | bytes 262144
  1.0 1.1 %multiply_dynamic-update-slice_fusion.2 = (f32[5,8,32,128]{3,2,1,0:T(8,128)S(1)}, f32[1,8,32,128]{3,2,1,0:T(8,128)S(1)}) fusion(f32[5,8,32,128]{3,2,1,0:T(8,128)S(1)} %slice_dynamic-update-slice_fusion, f32[5,8,32,128]{3,2,1,0:T(8,128)} %param.9), kind=kLoop, calls=%fused_computation.83 | loop fusion | flops 65536 | bytes 655360
  2.9 3.4 %collective-permute-start.2 = (f32[5,8,4,128]{3,1,2,0:T(8,128)S(1)}, f32[5,8,4,128]{3,1,2,0:T(8,128)S(1)}, u32[]{:S(2)}, u32[]{:S(2)}) collective-permute-start(f32[5,8,4,128]{3,1,2,0:T(8,128)S(1)} %copy.68), channel_id=1, source_target_pairs={{0,4},{4,8},{8,12},{1,5},{5,9},{9,13},{2,6},{6,10},{10,14},{3,7},{... | collective-permute-start | bytes 245768 | tf_op jit(solution)/shard_map/ppermute | solution.py:23
  6.3 3.5 %collective-permute-start.3 = (f32[5,8,4,128]{3,1,2,0:T(8,128)S(1)}, f32[5,8,4,128]{3,1,2,0:T(8,128)S(1)}, u32[]{:S(2)}, u32[]{:S(2)}) collective-permute-start(f32[5,8,4,128]{3,1,2,0:T(8,128)S(1)} %copy.69), channel_id=1, source_target_pairs={{4,0},{8,4},{12,8},{5,1},{9,5},{13,9},{6,2},{10,6},{14,10},{7,3},{... | collective-permute-start | bytes 245768 | tf_op jit(solution)/shard_map/ppermute | solution.py:25
  9.8 1.0 %fusion.111 = f32[1,5,32,128]{3,0,2,1:T(1,128)S(1)} fusion(f32[5,8,32,128]{3,2,1,0:T(8,128)S(1)} %copy-done), kind=kOutput, calls=%fused_computation.179 | convolution fusion | flops 1966096 | bytes 737280 | tf_op jit(solution)/shard_map/j,fjas->fas/dot_general | solution.py:106
  10.8 1.0 %fusion.88 = f32[1,5,32,128]{3,0,2,1:T(1,128)S(1)} fusion(f32[5,8,32,128]{3,2,1,0:T(8,128)S(1)} %copy-done), kind=kOutput, calls=%fused_computation.159 | convolution fusion | flops 1966088 | bytes 737280 | tf_op jit(solution)/shard_map/j,fjas->fas/dot_general | solution.py:112
  13.2 1.0 %fusion.41 = f32[1,5,32,128]{3,0,2,1:T(1,128)S(1)} fusion(f32[5,8,32,128]{3,2,1,0:T(8,128)S(1)} %fusion.50), kind=kOutput, calls=%fused_computation.66 | convolution fusion | flops 1966216 | bytes 737280 | tf_op jit(solution)/shard_map/j,fjas->fas/dot_general | solution.py:106
  14.2 1.0 %fusion.39 = f32[1,5,32,128]{3,0,2,1:T(1,128)S(1)} fusion(f32[5,8,32,128]{3,2,1,0:T(8,128)S(1)} %fusion.50), kind=kOutput, calls=%fused_computation.64 | convolution fusion | flops 1966168 | bytes 737280 | tf_op jit(solution)/shard_map/j,fjas->fas/dot_general | solution.py:112
  15.2 2.0 %all-gather = f32[4,5,32,128]{3,2,1,0:T(8,128)S(1)} all-gather(f32[2,5,32,128]{3,2,1,0:T(8,128)S(1)} %pad_maximum_fusion.4), channel_id=2, replica_groups=mesh['pitch'=2,'axial'=4,'span'=4] {'pitch'}, dimensions={0}, use_global_device_ids=true | all-gather | bytes 491520 | tf_op jit(solution)/shard_map/all_gather | solution.py:168
  17.2 2.0 %all-gather.1 = f32[4,5,32,128]{3,2,1,0:T(8,128)S(1)} all-gather(f32[2,5,32,128]{3,2,1,0:T(8,128)S(1)} %pad_maximum_fusion.5), channel_id=3, replica_groups=mesh['pitch'=2,'axial'=4,'span'=4] {'pitch'}, dimensions={0}, use_global_device_ids=true | all-gather | bytes 491520 | tf_op jit(solution)/shard_map/all_gather | solution.py:169
  19.3 1.3 %fusion.48 = f32[2,1,5,32,128]{4,1,3,2,0:T(1,128)S(1)} fusion(f32[2,2,1,1,1]{0,2,4,3,1:T(1,128)S(1)} %copy.37, f32[2,2,5,32,128]{4,3,2,1,0:T(8,128)S(1)} %bitcast.111), kind=kOutput, calls=%fused_computation.75 | convolution fusion | flops 983040 | bytes 491536 | tf_op jit(solution)/shard_map/er,erfas->rfas/dot_general | solution.py:178
  20.6 1.3 %fusion.46 = f32[2,1,5,32,128]{4,1,3,2,0:T(1,128)S(1)} fusion(f32[2,2,1,1,1]{0,2,4,3,1:T(1,128)S(1)} %copy.44, f32[2,2,5,32,128]{4,3,2,1,0:T(8,128)S(1)} %bitcast.112), kind=kOutput, calls=%fused_computation.73 | convolution fusion | flops 983040 | bytes 491536 | tf_op jit(solution)/shard_map/er,erfas->rfas/dot_general | solution.py:181
  21.9 0.6 %constant_dynamic-update-slice_fusion.1 = (f32[5,8,36,128]{3,1,2,0:T(8,128)}, f32[5,8,40,128]{3,1,2,0:T(8,128)S(1)}) fusion(f32[5,8,4,128]{3,1,2,0:T(8,128)S(1)} %collective-permute-done.2), kind=kLoop, calls=%fused_computation.97 | loop fusion | bytes 245760
  22.6 1.6 %constant_dynamic-update-slice_fusion = (f32[5,8,36,128]{3,1,2,0:T(8,128)}, f32[5,8,36,128]{3,1,2,0:T(8,128)}, f32[5,8,40,128]{3,1,2,0:T(8,128)S(1)}) fusion(f32[5,8,36,128]{3,1,2,0:T(8,128)} %get-tuple-element.48, f32[5,8,32,128]{3,2,1,0:T(8,128)S(1)} %copy-done, f32[5,8,40,128]{3,1,2,0:T(8,128)S(1)} %get-tuple-element.49), kind=kLoop, calls=%fused_computation.96 | loop fusion | bytes 2621440 | tf_op jit(solution)/shard_map/concatenate | solution.py:21
  24.2 0.6 %constant_dynamic-update-slice_fusion.2 = (f32[5,8,36,128]{3,1,2,0:T(8,128)}, f32[5,8,40,128]{3,1,2,0:T(8,128)S(1)}) fusion(f32[5,8,36,128]{3,1,2,0:T(8,128)} %get-tuple-element.40, f32[5,8,4,128]{3,1,2,0:T(8,128)S(1)} %collective-permute-done.3, f32[5,8,40,128]{3,1,2,0:T(8,128)S(1)} %get-tuple-element.41), kind=kLoop, calls=%fused_computation.98 | loop fusion | bytes 245760 | tf_op jit(solution)/shard_map/concatenate | solution.py:21
  24.8 1.2 %fusion.152 = (f32[5,8,40,4]{3,1,2,0:T(8,128)}, f32[5,8,40,4]{3,1,2,0:T(8,128)S(1)}) fusion(f32[5,8,40,128]{3,1,2,0:T(8,128)S(1)} %get-tuple-element.51), kind=kLoop, calls=%fused_computation.227 | loop fusion | bytes 102400 | tf_op jit(solution)/shard_map/slice | solution.py:20
  26.0 1.5 %copy.27 = f32[5,8,40,4]{2,1,3,0:T(8,128)S(1)} copy(f32[5,8,40,4]{3,1,2,0:T(8,128)} %get-tuple-element.35) | data formatting | bytes 51200 | tf_op jit(solution)/shard_map/slice | solution.py:20
  27.5 3.5 %collective-permute-start.4 = (f32[5,8,40,4]{2,1,3,0:T(8,128)S(1)}, f32[5,8,40,4]{2,1,3,0:T(8,128)S(1)}, u32[]{:S(2)}, u32[]{:S(2)}) collective-permute-start(f32[5,8,40,4]{2,1,3,0:T(8,128)S(1)} %copy.27), channel_id=1, source_target_pairs={{0,1},{1,2},{2,3},{4,5},{5,6},{6,7},{8,9},{9,10},{10,11},{12,13},{... | collective-permute-start | bytes 76808 | tf_op jit(solution)/shard_map/ppermute | solution.py:23
  31.3 2.5 %collective-permute-start.5 = (f32[5,8,40,4]{2,1,3,0:T(8,128)S(1)}, f32[5,8,40,4]{2,1,3,0:T(8,128)}, u32[]{:S(2)}, u32[]{:S(2)}) collective-permute-start(f32[5,8,40,4]{2,1,3,0:T(8,128)S(1)} %copy.29), channel_id=1, source_target_pairs={{1,0},{2,1},{3,2},{5,4},{6,5},{7,6},{9,8},{10,9},{11,10},{13,12},{... | collective-permute-start | bytes 76808 | tf_op jit(solution)/shard_map/ppermute | solution.py:25
  33.9 2.0 %fusion.6 = f32[5,8,32,128]{3,1,2,0:T(8,128)} fusion(f32[5,8,32,128]{3,2,1,0:T(8,128)S(1)} %fusion.50, f32[5,32,128]{2,1,0:T(8,128)S(1)} %get-tuple-element.47, f32[8]{0:T(128)S(1)} %get-tuple-element.59, f32[5,32,128]{2,1,0:T(8,128)S(1)} %get-tuple-element.45, f32[8]{0:T(128)S(1)} %get-tuple-element.58), kind=kOutput, calls=%fused_computation.20 | convolution fusion | flops 16548992 | bytes 1474624 | tf_op jit(solution)/shard_map/ij,fjas->fias/dot_general | solution.py:131
  36.2 1.5 %collective-permute-done.5 = f32[5,8,40,4]{2,1,3,0:T(8,128)} collective-permute-done((f32[5,8,40,4]{2,1,3,0:T(8,128)S(1)}, f32[5,8,40,4]{2,1,3,0:T(8,128)}, u32[]{:S(2)}, u32[]{:S(2)}) %collective-permute-start.5) | collective-permute-done | bytes 25632 | tf_op jit(solution)/shard_map/ppermute | solution.py:25
  37.8 2.1 %copy.30 = f32[5,8,40,4]{3,1,2,0:T(8,128)} copy(f32[5,8,40,4]{2,1,3,0:T(8,128)} %collective-permute-done.5) | data formatting | bytes 51200 | tf_op jit(solution)/shard_map/ppermute | solution.py:25
  39.9 6.2 %fusion.13 = f32[5,8,32,128]{3,1,2,0:T(8,128)S(1)} fusion(f32[5,8,40,128]{3,1,2,0:T(8,128)S(1)} %get-tuple-element.51, f32[5,8,40,4]{3,1,2,0:T(8,128)} %copy.30, f32[5,8,40,4]{3,1,2,0:T(8,128)S(1)} %copy.28, f32[5,8,36,128]{3,1,2,0:T(8,128)} %get-tuple-element.50, f32[5,8,36,128]{3,1,2,0:T(8,128)} %get-tuple-element.39, ...), kind=kOutput, calls=%fused_computation.27 | convolution fusion | flops 23265472 | bytes 9693184 | tf_op jit(solution)/shard_map/ij,fjas->fias/dot_general | solution.py:131
  46.1 1.0 %copy.31 = f32[5,8,32,128]{3,2,1,0:T(8,128)} copy(f32[5,8,32,128]{3,1,2,0:T(8,128)S(1)} %fusion.13) | data formatting | bytes 1310720 | tf_op jit(solution)/shard_map/sub | solution.py:191
  (43 shorter events, 2.2 us)
Async XLA Ops:
  0.0 2.1 %copy-start = (f32[5,8,32,128]{3,2,1,0:T(8,128)S(1)}, f32[5,8,32,128]{3,2,1,0:T(8,128)}, u32[]{:S(2)}) copy-start(f32[5,8,32,128]{3,2,1,0:T(8,128)} %param.9) | copy-start | bytes 1966084
  2.2 10.7 %collective-permute-start = (f32[5,1,32,128]{3,2,1,0:T(8,128)S(1)}, f32[5,1,32,128]{3,2,1,0:T(8,128)S(1)}, u32[]{:S(2)}, u32[]{:S(2)}) collective-permute-start(f32[5,1,32,128]{3,2,1,0:T(8,128)S(1)} %get-tuple-element.37), channel_id=1, source_target_pairs={{16,0},{0,16},{17,1},{1,17},{18,2},{2,18},{19,3},{3,19},{20,4},{4,... | collective-permute-start | bytes 245768 | tf_op jit(solution)/shard_map/ppermute | solution.py:25
  2.3 10.7 %collective-permute-start.1 = (f32[5,1,32,128]{3,2,1,0:T(8,128)S(1)}, f32[5,1,32,128]{3,2,1,0:T(8,128)S(1)}, u32[]{:S(2)}, u32[]{:S(2)}) collective-permute-start(f32[5,1,32,128]{3,2,1,0:T(8,128)S(1)} %get-tuple-element.38), channel_id=1, source_target_pairs={{0,16},{16,0},{1,17},{17,1},{2,18},{18,2},{3,19},{19,3},{4,20},{20... | collective-permute-start | bytes 245768 | tf_op jit(solution)/shard_map/ppermute | solution.py:23
  2.9 19.0 %collective-permute-start.2 = (f32[5,8,4,128]{3,1,2,0:T(8,128)S(1)}, f32[5,8,4,128]{3,1,2,0:T(8,128)S(1)}, u32[]{:S(2)}, u32[]{:S(2)}) collective-permute-start(f32[5,8,4,128]{3,1,2,0:T(8,128)S(1)} %copy.68), channel_id=1, source_target_pairs={{0,4},{4,8},{8,12},{1,5},{5,9},{9,13},{2,6},{6,10},{10,14},{3,7},{... | collective-permute-start | bytes 245768 | tf_op jit(solution)/shard_map/ppermute | solution.py:23
  6.3 6.3 %copy-start.4 = (f32[2]{0:T(128)S(1)}, f32[2]{0:T(128)}, u32[]{:S(2)}) copy-start(f32[2]{0:T(128)} %constant.173.clone) | copy-start | bytes 28
  6.3 6.5 %copy-start.3 = (s32[128]{0:T(128)S(1)}, s32[128]{0:T(128)}, u32[]{:S(2)}) copy-start(s32[128]{0:T(128)} %param.12) | copy-start | bytes 1540
  6.3 6.6 %copy-start.1 = (f32[2,4,5,32,128]{4,3,2,1,0:T(8,128)S(1)}, f32[2,4,5,32,128]{4,3,2,1,0:T(8,128)}, u32[]{:S(2)}) copy-start(f32[2,4,5,32,128]{4,3,2,1,0:T(8,128)} %param.10) | copy-start | bytes 1966084
  6.3 17.9 %collective-permute-start.3 = (f32[5,8,4,128]{3,1,2,0:T(8,128)S(1)}, f32[5,8,4,128]{3,1,2,0:T(8,128)S(1)}, u32[]{:S(2)}, u32[]{:S(2)}) collective-permute-start(f32[5,8,4,128]{3,1,2,0:T(8,128)S(1)} %copy.69), channel_id=1, source_target_pairs={{4,0},{8,4},{12,8},{5,1},{9,5},{13,9},{6,2},{10,6},{14,10},{7,3},{... | collective-permute-start | bytes 245768 | tf_op jit(solution)/shard_map/ppermute | solution.py:25
  27.5 8.4 %collective-permute-start.4 = (f32[5,8,40,4]{2,1,3,0:T(8,128)S(1)}, f32[5,8,40,4]{2,1,3,0:T(8,128)S(1)}, u32[]{:S(2)}, u32[]{:S(2)}) collective-permute-start(f32[5,8,40,4]{2,1,3,0:T(8,128)S(1)} %copy.27), channel_id=1, source_target_pairs={{0,1},{1,2},{2,3},{4,5},{5,6},{6,7},{8,9},{9,10},{10,11},{12,13},{... | collective-permute-start | bytes 76808 | tf_op jit(solution)/shard_map/ppermute | solution.py:23
  31.3 6.4 %collective-permute-start.5 = (f32[5,8,40,4]{2,1,3,0:T(8,128)S(1)}, f32[5,8,40,4]{2,1,3,0:T(8,128)}, u32[]{:S(2)}, u32[]{:S(2)}) collective-permute-start(f32[5,8,40,4]{2,1,3,0:T(8,128)S(1)} %copy.29), channel_id=1, source_target_pairs={{1,0},{2,1},{3,2},{5,4},{6,5},{7,6},{9,8},{10,9},{11,10},{13,12},{... | collective-permute-start | bytes 76808 | tf_op jit(solution)/shard_map/ppermute | solution.py:25
  35.9 4.0 %copy-start.2 = (f32[5,8,32,128]{3,1,2,0:T(8,128)S(1)}, f32[5,8,32,128]{3,1,2,0:T(8,128)}, u32[]{:S(2)}) copy-start(f32[5,8,32,128]{3,1,2,0:T(8,128)} %fusion.6) | copy-start | bytes 1966084
where the time goes:
time: 47.4 us; the launch traced here: 47 us
  matrix products  14.6 us (31%)
  starting transfers between devices  13.5 us (28%)
  local copies, waits for them, and re-layouts  10.6 us (22%)
  blocking collectives  4.08 us (9%)
  other arithmetic  1.7 us (4%)
  waiting for transfers between devices  1.55 us (3%)
  between operations  0.96 us (2%)
    dot_general x2, matrix products, finish(): jnp.einsum('ij,fjas->fias', kernel, values, precision=lax.Precision.HIGHEST)  8.15 us
    ppermute x3, starting transfers between devices, padded(): lax.ppermute(tail, axis, [(i, (i + 1) % count) for i in range(ends)])  7.38 us
    ppermute x3, starting transfers between devices, padded(): lax.ppermute(head, axis, [((i + 1) % count, i) for i in range(ends)])  6.08 us
    slice x2, local copies, waits for them, and re-layouts, padded(): lax.slice_in_dim(cells, cells.shape[dim] - width, cells.shape[dim], axis=...  2.65 us
    concatenate x2, local copies, waits for them, and re-layouts, padded(): jnp.concatenate([lax.ppermute(tail, axis, [(i, (i + 1) % count) for i in...  2.25 us
    ppermute x1, local copies, waits for them, and re-layouts, padded(): lax.ppermute(head, axis, [((i + 1) % count, i) for i in range(ends)])  2.12 us
    all_gather x1, blocking collectives, shards(): lax.all_gather(tail_sums[None], 'pitch', axis=0, tiled=True)  2.04 us
    all_gather x1, blocking collectives, shards(): lax.all_gather(leading_partial_totals[None], 'pitch', axis=0, tiled=True)  2.04 us
  transfers between devices with their start and end apart: 6, of which 1 were waited for; matrix products, arithmetic and copies ran while one was open for 26% of the time, Pallas kernels for 0%

commit v1 on v0

--- a/solution.py
+++ b/solution.py
@@ -164,8 +164,17 @@
         [1.0 / (1.0 - step_decays[0] ** npitch), 1.0 / (1.0 - step_decays[1] ** npitch)],
         jnp.float32,
     )
+
+    def runs_drive(shard_axis, target):
+        return jnp.concatenate(
+            lax.all_to_all(
+                jnp.stack(lax.axis_size(shard_axis) * [target], axis=0), shard_axis, 0, 0
+            ),
+            axis=0,
+        )
+
     collected = (
-        lax.all_gather(tail_sums[None], "pitch", axis=0, tiled=True),
+        runs_drive("pitch", tail_sums[None]),
         lax.all_gather(leading_partial_totals[None], "pitch", axis=0, tiled=True),
     )
     others = jnp.arange(npitch)

time: 47.4 us -> 49.7 us (1.049)
  starting transfers between devices: 13.5 us -> 16.9 us
  blocking collectives: 4.08 us -> 2.16 us
  other arithmetic: 1.7 us -> 2.46 us
    all_to_all x0 -> x1, starting transfers between devices: none -> 3.46 us  [runs_drive(): lax.all_to_all(jnp.stack(lax.axis_size(shard_axis) * [target], axis=0), s...]
    all_gather x1 -> x0, blocking collectives: 2.04 us -> none  [shards(): lax.all_gather(tail_sums[None], 'pitch', axis=0, tiled=True)]
    another operation x1 -> x2, other arithmetic: 0.01 us -> 0.77 us  [runs_drive(): jnp.stack(lax.axis_size(shard_axis) * [target], axis=0)]
  transfers between devices with their start and end apart: 6 -> 7, of which waited for: 1 -> 1; matrix products, arithmetic and copies ran while one was open for 26% -> 26% of each run, Pallas kernels for 0% -> 0%
where the time goes in v1:
time: 49.7 us; the launch traced here: 49.4 us
  starting transfers between devices  16.9 us (34%)
  matrix products  14.6 us (29%)
  local copies, waits for them, and re-layouts  10.7 us (22%)
  other arithmetic  2.46 us (5%)
  blocking collectives  2.16 us (4%)
  waiting for transfers between devices  1.55 us (3%)
  between operations  0.97 us (2%)
    dot_general x2, matrix products, finish(): jnp.einsum('ij,fjas->fias', kernel, values, precision=lax.Precision.HIGHEST)  8.14 us
    ppermute x3, starting transfers between devices, padded(): lax.ppermute(tail, axis, [(i, (i + 1) % count) for i in range(ends)])  7.38 us
    ppermute x3, starting transfers between devices, padded(): lax.ppermute(head, axis, [((i + 1) % count, i) for i in range(ends)])  6.08 us
    all_to_all x1, starting transfers between devices, runs_drive(): lax.all_to_all(jnp.stack(lax.axis_size(shard_axis) * [target], axis=0), s...  3.46 us
    slice x2, local copies, waits for them, and re-layouts, padded(): lax.slice_in_dim(cells, cells.shape[dim] - width, cells.shape[dim], axis=...  2.66 us
    concatenate x2, local copies, waits for them, and re-layouts, padded(): jnp.concatenate([lax.ppermute(tail, axis, [(i, (i + 1) % count) for i in...  2.23 us
    all_gather x1, blocking collectives, shards(): lax.all_gather(leading_partial_totals[None], 'pitch', axis=0, tiled=True)  2.16 us
    ppermute x1, local copies, waits for them, and re-layouts, padded(): lax.ppermute(head, axis, [((i + 1) % count, i) for i in range(ends)])  2.13 us
  transfers between devices with their start and end apart: 7, of which 1 were waited for; matrix products, arithmetic and copies ran while one was open for 26% of the time, Pallas kernels for 0%

profile of v1, /device:TPU:12, one launch (start us, length us, event | category | flops | bytes accessed | tf_op | source)
XLA Modules:
  0.0 49.4 jit_solution(1108622383612066474)
XLA Ops:
  0.0 1.0 %slice_dynamic-update-slice_fusion = f32[5,8,32,128]{3,2,1,0:T(8,128)S(1)} fusion(f32[5,8,32,128]{3,2,1,0:T(8,128)} %param.9), kind=kLoop, calls=%fused_computation.86 | loop fusion | bytes 262144
  1.0 1.1 %multiply_dynamic-update-slice_fusion.2 = (f32[5,8,32,128]{3,2,1,0:T(8,128)S(1)}, f32[1,8,32,128]{3,2,1,0:T(8,128)S(1)}) fusion(f32[5,8,32,128]{3,2,1,0:T(8,128)S(1)} %slice_dynamic-update-slice_fusion, f32[5,8,32,128]{3,2,1,0:T(8,128)} %param.9), kind=kLoop, calls=%fused_computation.84 | loop fusion | flops 65536 | bytes 655360
  2.9 3.4 %collective-permute-start.2 = (f32[5,8,4,128]{3,1,2,0:T(8,128)S(1)}, f32[5,8,4,128]{3,1,2,0:T(8,128)S(1)}, u32[]{:S(2)}, u32[]{:S(2)}) collective-permute-start(f32[5,8,4,128]{3,1,2,0:T(8,128)S(1)} %copy.68), channel_id=1, source_target_pairs={{0,4},{4,8},{8,12},{1,5},{5,9},{9,13},{2,6},{6,10},{10,14},{3,7},{... | collective-permute-start | bytes 245768 | tf_op jit(solution)/shard_map/ppermute | solution.py:23
  6.3 3.5 %collective-permute-start.3 = (f32[5,8,4,128]{3,1,2,0:T(8,128)S(1)}, f32[5,8,4,128]{3,1,2,0:T(8,128)S(1)}, u32[]{:S(2)}, u32[]{:S(2)}) collective-permute-start(f32[5,8,4,128]{3,1,2,0:T(8,128)S(1)} %copy.69), channel_id=1, source_target_pairs={{4,0},{8,4},{12,8},{5,1},{9,5},{13,9},{6,2},{10,6},{14,10},{7,3},{... | collective-permute-start | bytes 245768 | tf_op jit(solution)/shard_map/ppermute | solution.py:25
  9.8 1.0 %fusion.111 = f32[1,5,32,128]{3,0,2,1:T(1,128)S(1)} fusion(f32[5,8,32,128]{3,2,1,0:T(8,128)S(1)} %copy-done), kind=kOutput, calls=%fused_computation.180 | convolution fusion | flops 1966096 | bytes 737280 | tf_op jit(solution)/shard_map/j,fjas->fas/dot_general | solution.py:106
  10.8 1.0 %fusion.88 = f32[1,5,32,128]{3,0,2,1:T(1,128)S(1)} fusion(f32[5,8,32,128]{3,2,1,0:T(8,128)S(1)} %copy-done), kind=kOutput, calls=%fused_computation.160 | convolution fusion | flops 1966088 | bytes 737280 | tf_op jit(solution)/shard_map/j,fjas->fas/dot_general | solution.py:112
  13.2 1.0 %fusion.41 = f32[1,5,32,128]{3,0,2,1:T(1,128)S(1)} fusion(f32[5,8,32,128]{3,2,1,0:T(8,128)S(1)} %fusion.50), kind=kOutput, calls=%fused_computation.66 | convolution fusion | flops 1966216 | bytes 737280 | tf_op jit(solution)/shard_map/j,fjas->fas/dot_general | solution.py:106
  14.2 1.0 %fusion.39 = f32[1,5,32,128]{3,0,2,1:T(1,128)S(1)} fusion(f32[5,8,32,128]{3,2,1,0:T(8,128)S(1)} %fusion.50), kind=kOutput, calls=%fused_computation.64 | convolution fusion | flops 1966168 | bytes 737280 | tf_op jit(solution)/shard_map/j,fjas->fas/dot_general | solution.py:112
  15.2 0.8 %pad_maximum_fusion.4 = f32[2,1,2,5,32,128]{5,4,3,2,1,0:T(8,128)} fusion(f32[1,1,2,5,32,128]{5,4,3,2,1,0:T(8,128)S(1)} %maximum_bitcast_fusion), kind=kLoop, calls=%fused_computation.69 | loop fusion | flops 81920 | bytes 491520 | tf_op jit(solution)/shard_map/stack | solution.py:171
  15.9 3.5 %all-to-all-start = ((f32[2,1,2,5,32,128]{5,4,3,2,1,0:T(8,128)}), f32[2,1,2,5,32,128]{5,4,3,2,1,0:T(8,128)S(1)}, u32[]{:S(2)}, u32[]{:S(2)}) async-start(f32[2,1,2,5,32,128]{5,4,3,2,1,0:T(8,128)} %pad_maximum_fusion.4), calls=%async_computation | async-start | bytes 655360 | tf_op jit(solution)/shard_map/all_to_all | solution.py:170
  19.4 2.2 %all-gather = f32[4,5,32,128]{3,2,1,0:T(8,128)S(1)} all-gather(f32[2,5,32,128]{3,2,1,0:T(8,128)S(1)} %pad_maximum_fusion.5), channel_id=2, replica_groups=mesh['pitch'=2,'axial'=4,'span'=4] {'pitch'}, dimensions={0}, use_global_device_ids=true | all-gather | bytes 491520 | tf_op jit(solution)/shard_map/all_gather | solution.py:178
  21.6 1.3 %fusion.48 = f32[2,1,5,32,128]{4,1,3,2,0:T(1,128)S(1)} fusion(f32[2,2,1,1,1]{0,2,4,3,1:T(1,128)S(1)} %copy.37, f32[2,2,5,32,128]{4,3,2,1,0:T(8,128)S(1)} %bitcast.113), kind=kOutput, calls=%fused_computation.76 | convolution fusion | flops 983040 | bytes 491536 | tf_op jit(solution)/shard_map/er,erfas->rfas/dot_general | solution.py:187
  22.9 1.3 %fusion.46 = f32[2,1,5,32,128]{4,1,3,2,0:T(1,128)S(1)} fusion(f32[2,2,1,1,1]{0,2,4,3,1:T(1,128)S(1)} %copy.44, f32[2,2,5,32,128]{4,3,2,1,0:T(8,128)S(1)} %bitcast.114), kind=kOutput, calls=%fused_computation.74 | convolution fusion | flops 983040 | bytes 491536 | tf_op jit(solution)/shard_map/er,erfas->rfas/dot_general | solution.py:190
  24.2 0.7 %constant_dynamic-update-slice_fusion.1 = (f32[5,8,36,128]{3,1,2,0:T(8,128)}, f32[5,8,40,128]{3,1,2,0:T(8,128)S(1)}) fusion(f32[5,8,4,128]{3,1,2,0:T(8,128)S(1)} %collective-permute-done.2), kind=kLoop, calls=%fused_computation.98 | loop fusion | bytes 245760
  24.9 1.6 %constant_dynamic-update-slice_fusion = (f32[5,8,36,128]{3,1,2,0:T(8,128)}, f32[5,8,36,128]{3,1,2,0:T(8,128)}, f32[5,8,40,128]{3,1,2,0:T(8,128)S(1)}) fusion(f32[5,8,36,128]{3,1,2,0:T(8,128)} %get-tuple-element.48, f32[5,8,32,128]{3,2,1,0:T(8,128)S(1)} %copy-done, f32[5,8,40,128]{3,1,2,0:T(8,128)S(1)} %get-tuple-element.49), kind=kLoop, calls=%fused_computation.97 | loop fusion | bytes 2621440 | tf_op jit(solution)/shard_map/concatenate | solution.py:21
  27.1 1.2 %fusion.152 = (f32[5,8,40,4]{3,1,2,0:T(8,128)}, f32[5,8,40,4]{3,1,2,0:T(8,128)S(1)}) fusion(f32[5,8,40,128]{3,1,2,0:T(8,128)S(1)} %get-tuple-element.51), kind=kLoop, calls=%fused_computation.228 | loop fusion | bytes 102400 | tf_op jit(solution)/shard_map/slice | solution.py:20
  28.3 1.5 %copy.27 = f32[5,8,40,4]{2,1,3,0:T(8,128)S(1)} copy(f32[5,8,40,4]{3,1,2,0:T(8,128)} %get-tuple-element.35) | data formatting | bytes 51200 | tf_op jit(solution)/shard_map/slice | solution.py:20
  29.8 3.5 %collective-permute-start.4 = (f32[5,8,40,4]{2,1,3,0:T(8,128)S(1)}, f32[5,8,40,4]{2,1,3,0:T(8,128)S(1)}, u32[]{:S(2)}, u32[]{:S(2)}) collective-permute-start(f32[5,8,40,4]{2,1,3,0:T(8,128)S(1)} %copy.27), channel_id=1, source_target_pairs={{0,1},{1,2},{2,3},{4,5},{5,6},{6,7},{8,9},{9,10},{10,11},{12,13},{... | collective-permute-start | bytes 76808 | tf_op jit(solution)/shard_map/ppermute | solution.py:23
  33.6 2.5 %collective-permute-start.5 = (f32[5,8,40,4]{2,1,3,0:T(8,128)S(1)}, f32[5,8,40,4]{2,1,3,0:T(8,128)}, u32[]{:S(2)}, u32[]{:S(2)}) collective-permute-start(f32[5,8,40,4]{2,1,3,0:T(8,128)S(1)} %copy.29), channel_id=1, source_target_pairs={{1,0},{2,1},{3,2},{5,4},{6,5},{7,6},{9,8},{10,9},{11,10},{13,12},{... | collective-permute-start | bytes 76808 | tf_op jit(solution)/shard_map/ppermute | solution.py:25
  36.2 2.0 %fusion.6 = f32[5,8,32,128]{3,1,2,0:T(8,128)} fusion(f32[5,8,32,128]{3,2,1,0:T(8,128)S(1)} %fusion.50, f32[5,32,128]{2,1,0:T(8,128)S(1)} %get-tuple-element.47, f32[8]{0:T(128)S(1)} %get-tuple-element.59, f32[5,32,128]{2,1,0:T(8,128)S(1)} %get-tuple-element.45, f32[8]{0:T(128)S(1)} %get-tuple-element.58), kind=kOutput, calls=%fused_computation.20 | convolution fusion | flops 16548992 | bytes 1474624 | tf_op jit(solution)/shard_map/ij,fjas->fias/dot_general | solution.py:131
  38.6 1.5 %collective-permute-done.5 = f32[5,8,40,4]{2,1,3,0:T(8,128)} collective-permute-done((f32[5,8,40,4]{2,1,3,0:T(8,128)S(1)}, f32[5,8,40,4]{2,1,3,0:T(8,128)}, u32[]{:S(2)}, u32[]{:S(2)}) %collective-permute-start.5) | collective-permute-done | bytes 25632 | tf_op jit(solution)/shard_map/ppermute | solution.py:25
  40.1 2.1 %copy.30 = f32[5,8,40,4]{3,1,2,0:T(8,128)} copy(f32[5,8,40,4]{2,1,3,0:T(8,128)} %collective-permute-done.5) | data formatting | bytes 51200 | tf_op jit(solution)/shard_map/ppermute | solution.py:25
  42.2 6.2 %fusion.13 = f32[5,8,32,128]{3,1,2,0:T(8,128)S(1)} fusion(f32[5,8,40,128]{3,1,2,0:T(8,128)S(1)} %get-tuple-element.51, f32[5,8,40,4]{3,1,2,0:T(8,128)} %copy.30, f32[5,8,40,4]{3,1,2,0:T(8,128)S(1)} %copy.28, f32[5,8,36,128]{3,1,2,0:T(8,128)} %get-tuple-element.50, f32[5,8,36,128]{3,1,2,0:T(8,128)} %get-tuple-element.39, ...), kind=kOutput, calls=%fused_computation.27 | convolution fusion | flops 23265472 | bytes 9693184 | tf_op jit(solution)/shard_map/ij,fjas->fias/dot_general | solution.py:131
  48.4 1.0 %copy.31 = f32[5,8,32,128]{3,2,1,0:T(8,128)} copy(f32[5,8,32,128]{3,1,2,0:T(8,128)S(1)} %fusion.13) | data formatting | bytes 1310720 | tf_op jit(solution)/shard_map/sub | solution.py:200
  (45 shorter events, 2.9 us)
Async XLA Ops:
  0.0 2.1 %copy-start = (f32[5,8,32,128]{3,2,1,0:T(8,128)S(1)}, f32[5,8,32,128]{3,2,1,0:T(8,128)}, u32[]{:S(2)}) copy-start(f32[5,8,32,128]{3,2,1,0:T(8,128)} %param.9) | copy-start | bytes 1966084
  2.2 10.7 %collective-permute-start = (f32[5,1,32,128]{3,2,1,0:T(8,128)S(1)}, f32[5,1,32,128]{3,2,1,0:T(8,128)S(1)}, u32[]{:S(2)}, u32[]{:S(2)}) collective-permute-start(f32[5,1,32,128]{3,2,1,0:T(8,128)S(1)} %get-tuple-element.37), channel_id=1, source_target_pairs={{16,0},{0,16},{17,1},{1,17},{18,2},{2,18},{19,3},{3,19},{20,4},{4,... | collective-permute-start | bytes 245768 | tf_op jit(solution)/shard_map/ppermute | solution.py:25
  2.3 10.7 %collective-permute-start.1 = (f32[5,1,32,128]{3,2,1,0:T(8,128)S(1)}, f32[5,1,32,128]{3,2,1,0:T(8,128)S(1)}, u32[]{:S(2)}, u32[]{:S(2)}) collective-permute-start(f32[5,1,32,128]{3,2,1,0:T(8,128)S(1)} %get-tuple-element.38), channel_id=1, source_target_pairs={{0,16},{16,0},{1,17},{17,1},{2,18},{18,2},{3,19},{19,3},{4,20},{20... | collective-permute-start | bytes 245768 | tf_op jit(solution)/shard_map/ppermute | solution.py:23
  2.9 21.4 %collective-permute-start.2 = (f32[5,8,4,128]{3,1,2,0:T(8,128)S(1)}, f32[5,8,4,128]{3,1,2,0:T(8,128)S(1)}, u32[]{:S(2)}, u32[]{:S(2)}) collective-permute-start(f32[5,8,4,128]{3,1,2,0:T(8,128)S(1)} %copy.68), channel_id=1, source_target_pairs={{0,4},{4,8},{8,12},{1,5},{5,9},{9,13},{2,6},{6,10},{10,14},{3,7},{... | collective-permute-start | bytes 245768 | tf_op jit(solution)/shard_map/ppermute | solution.py:23
  6.3 6.3 %copy-start.4 = (f32[2]{0:T(128)S(1)}, f32[2]{0:T(128)}, u32[]{:S(2)}) copy-start(f32[2]{0:T(128)} %constant.173.clone) | copy-start | bytes 28
  6.3 6.5 %copy-start.3 = (s32[128]{0:T(128)S(1)}, s32[128]{0:T(128)}, u32[]{:S(2)}) copy-start(s32[128]{0:T(128)} %param.12) | copy-start | bytes 1540
  6.3 6.6 %copy-start.1 = (f32[2,4,5,32,128]{4,3,2,1,0:T(8,128)S(1)}, f32[2,4,5,32,128]{4,3,2,1,0:T(8,128)}, u32[]{:S(2)}) copy-start(f32[2,4,5,32,128]{4,3,2,1,0:T(8,128)} %param.10) | copy-start | bytes 1966084
  6.3 20.2 %collective-permute-start.3 = (f32[5,8,4,128]{3,1,2,0:T(8,128)S(1)}, f32[5,8,4,128]{3,1,2,0:T(8,128)S(1)}, u32[]{:S(2)}, u32[]{:S(2)}) collective-permute-start(f32[5,8,4,128]{3,1,2,0:T(8,128)S(1)} %copy.69), channel_id=1, source_target_pairs={{4,0},{8,4},{12,8},{5,1},{9,5},{13,9},{6,2},{10,6},{14,10},{7,3},{... | collective-permute-start | bytes 245768 | tf_op jit(solution)/shard_map/ppermute | solution.py:25
  15.9 5.6 %all-to-all-start = ((f32[2,1,2,5,32,128]{5,4,3,2,1,0:T(8,128)}), f32[2,1,2,5,32,128]{5,4,3,2,1,0:T(8,128)S(1)}, u32[]{:S(2)}, u32[]{:S(2)}) async-start(f32[2,1,2,5,32,128]{5,4,3,2,1,0:T(8,128)} %pad_maximum_fusion.4), calls=%async_computation | async-start | bytes 655360 | tf_op jit(solution)/shard_map/all_to_all | solution.py:170
  29.8 8.4 %collective-permute-start.4 = (f32[5,8,40,4]{2,1,3,0:T(8,128)S(1)}, f32[5,8,40,4]{2,1,3,0:T(8,128)S(1)}, u32[]{:S(2)}, u32[]{:S(2)}) collective-permute-start(f32[5,8,40,4]{2,1,3,0:T(8,128)S(1)} %copy.27), channel_id=1, source_target_pairs={{0,1},{1,2},{2,3},{4,5},{5,6},{6,7},{8,9},{9,10},{10,11},{12,13},{... | collective-permute-start | bytes 76808 | tf_op jit(solution)/shard_map/ppermute | solution.py:23
  33.6 6.4 %collective-permute-start.5 = (f32[5,8,40,4]{2,1,3,0:T(8,128)S(1)}, f32[5,8,40,4]{2,1,3,0:T(8,128)}, u32[]{:S(2)}, u32[]{:S(2)}) collective-permute-start(f32[5,8,40,4]{2,1,3,0:T(8,128)S(1)} %copy.29), channel_id=1, source_target_pairs={{1,0},{2,1},{3,2},{5,4},{6,5},{7,6},{9,8},{10,9},{11,10},{13,12},{... | collective-permute-start | bytes 76808 | tf_op jit(solution)/shard_map/ppermute | solution.py:25
  38.2 4.1 %copy-start.2 = (f32[5,8,32,128]{3,1,2,0:T(8,128)S(1)}, f32[5,8,32,128]{3,1,2,0:T(8,128)}, u32[]{:S(2)}) copy-start(f32[5,8,32,128]{3,1,2,0:T(8,128)} %fusion.6) | copy-start | bytes 1966084
